TPU v7x, 32 devices: a whole 2x2x4 slice. The times are simulated.
32 devices in a mesh: seq: 4 (over y, x), fsdp: 8 (over z, core).
Axes of the slice: x: 2, y: 2, z: 4, core: 2. Of those that a mesh axis runs over, the one named last changes fastest.
Arguments:
- tokens: bfloat16 [8, 1024, 1280], P('fsdp', 'seq'), may hold values from -6 to 6
- picture_ids: int32 [8, 1024], P('fsdp', 'seq'), may hold values from -1 to 10, as said below
- patch_rows: int32 [8, 1024], P('fsdp', 'seq'), may hold values from 0 to 31, as said below
- patch_cols: int32 [8, 1024], P('fsdp', 'seq'), may hold values from 0 to 31, as said below
- norm1_gain: bfloat16 [1280], P('fsdp'), may hold values from 0.099609375 to 1.8984375
- norm1_bias: bfloat16 [1280], P('fsdp'), may hold values from -3 to 3
- qkv_weight: bfloat16 [1280, 3840], P('fsdp'), may hold values from -0.15625 to 0.15625
- qkv_bias: bfloat16 [3840], P('fsdp'), may hold values from -3 to 3
- proj_weight: bfloat16 [1280, 1280], P('fsdp'), may hold values from -2 to 2
- proj_bias: bfloat16 [1280], P('fsdp'), may hold values from -3 to 3
- norm2_gain: bfloat16 [1280], P('fsdp'), may hold values from 0.099609375 to 1.8984375
- norm2_bias: bfloat16 [1280], P('fsdp'), may hold values from -3 to 3
- fc1_weight: bfloat16 [1280, 5120], P('fsdp'), may hold values from -0.15625 to 0.15625
- fc1_bias: bfloat16 [5120], P('fsdp'), may hold values from -3 to 3
- fc2_weight: bfloat16 [5120, 1280], P('fsdp'), may hold values from -0.078125 to 0.078125
- fc2_bias: bfloat16 [1280], P('fsdp'), may hold values from -3 to 3
- cotangent: bfloat16 [8, 1024, 1280], P('fsdp', 'seq'), may hold values from -6 to 6
Outputs:
- block_out: bfloat16 [8, 1024, 1280], P('fsdp', 'seq')
- tokens_grad: float32 [8, 1024, 1280], P('fsdp', 'seq')
- norm1_gain_grad: float32 [1280], P('fsdp')
- norm1_bias_grad: float32 [1280], P('fsdp')
- qkv_weight_grad: float32 [1280, 3840], P('fsdp')
- qkv_bias_grad: float32 [3840], P('fsdp')
- proj_weight_grad: float32 [1280, 1280], P('fsdp')
- proj_bias_grad: float32 [1280], P('fsdp')
- norm2_gain_grad: float32 [1280], P('fsdp')
- norm2_bias_grad: float32 [1280], P('fsdp')
- fc1_weight_grad: float32 [1280, 5120], P('fsdp')
- fc1_bias_grad: float32 [5120], P('fsdp')
- fc2_weight_grad: float32 [5120, 1280], P('fsdp')
- fc2_bias_grad: float32 [1280], P('fsdp')
Inputs may be any that keep to these rules, and one draw needn't show every extreme that they name: `picture_ids`: each sequence holds whole pictures in turn from its first token: picture number p (0, 1, 2, ...) of h x w patches, h and w from 10 to 32, takes h * w consecutive tokens with id p; only the last picture of a sequence may have fewer than h rows of patches; the tokens after it, fewer than 32, are padding with id -1. The first sequence holds only pictures of 10 x 10 patches. `patch_rows`: the row of a token's patch within its picture, the picture's tokens going row after row; 0 on padding. The last sequence begins with a picture of 32 x 32 patches. `patch_cols`: the column of a token's patch within its picture; 0 on padding.
All inputs are finite; a program needn't handle non-finite values.
Results may differ from a plain program's by a relative error of at most 0.018.
Values may be sent and summed in bfloat16 or wider, within the bound.
A program may use at most 256 MiB of HBM per device.

v0:
```python
import jax
import jax.numpy as jnp
from jax import lax
from jax.sharding import PartitionSpec as P

HD = 80


NORM_EPSILON = 1e-06
MASKED = -1e30


def standardize(values_in):
    centre = jnp.mean(values_in, axis=-1, keepdims=True)
    shifted = values_in - centre
    factor = lax.rsqrt(jnp.mean(shifted * shifted, axis=-1, keepdims=True) + NORM_EPSILON)
    return (shifted * factor, factor)


def norm_back(grad_out, normed, factor, gain):
    scaled = grad_out * gain
    return factor * (
        scaled
        - jnp.mean(scaled, axis=-1, keepdims=True)
        - normed * jnp.mean(scaled * normed, axis=-1, keepdims=True)
    )


def rotary_tables(patch_row, patch_col, head_size):
    quarter = head_size // 4
    inverse = jnp.power(10000.0, -jnp.arange(quarter, dtype=jnp.float32) / quarter)
    half_angles = jnp.concatenate(
        [
            patch_row.astype(jnp.float32)[..., None] * inverse,
            patch_col.astype(jnp.float32)[..., None] * inverse,
        ],
        axis=-1,
    )
    angles = jnp.concatenate([half_angles, half_angles], axis=-1)
    return (jnp.cos(angles)[..., None, :], jnp.sin(angles)[..., None, :])


def rotate(values_in, cosine, sine):
    half_size = values_in.shape[-1] // 2
    turned = jnp.concatenate([-values_in[..., half_size:], values_in[..., :half_size]], axis=-1)
    return values_in * cosine + turned * sine


def unrotate(grad_in, cosine, sine):
    half_size = grad_in.shape[-1] // 2
    moved = grad_in * sine
    return grad_in * cosine + jnp.concatenate(
        [moved[..., half_size:], -moved[..., :half_size]], axis=-1
    )


def masked_scores(query_block, keys, picture_block, place_block, picture, factor):
    places = jnp.arange(picture.shape[0], dtype=jnp.int32)
    scores = (
        jnp.einsum("qhd,khd->hqk", query_block, keys, preferred_element_type=jnp.float32) * factor
    )
    allowed = (picture_block[:, None] == picture[None, :]) & (
        (picture[None, :] >= 0) | (place_block[:, None] == places[None, :])
    )
    return jnp.where(allowed[None, :, :], scores, MASKED)


def attend_row(pieces):
    queries, keys, values, picture = pieces
    length, local_heads, head_size = queries.shape
    block_len = min(512, length)
    block_count = length // block_len
    factor = head_size ** (-0.5)
    places = jnp.arange(length, dtype=jnp.int32)

    def one_block(block_in):
        query_block, picture_block, place_block = block_in
        scores = masked_scores(query_block, keys, picture_block, place_block, picture, factor)
        row_max = jnp.max(scores, axis=-1, keepdims=True)
        powers = jnp.exp(scores - row_max)
        totals = jnp.sum(powers, axis=-1, keepdims=True)
        weights = (powers / totals).astype(jnp.bfloat16)
        mixed = jnp.einsum("hqk,khd->qhd", weights, values, preferred_element_type=jnp.float32)
        return (mixed, (row_max + jnp.log(totals))[..., 0])

    block_in = (
        queries.reshape(block_count, block_len, local_heads, head_size),
        picture.reshape(block_count, block_len),
        places.reshape(block_count, block_len),
    )
    mixed, log_total = lax.map(one_block, block_in)
    return (mixed.reshape(length, local_heads, head_size), log_total)


def attend_back(pieces):
    queries, keys, values, picture, grad_mixed, log_total = pieces
    length, local_heads, head_size = queries.shape
    block_len = min(512, length)
    block_count = length // block_len
    factor = head_size ** (-0.5)
    places = jnp.arange(length, dtype=jnp.int32)

    def one_block(carry, block_in):
        grad_keys, grad_values = carry
        query_block, picture_block, place_block, grad_block, log_block = block_in
        scores = masked_scores(query_block, keys, picture_block, place_block, picture, factor)
        probs_full = jnp.exp(scores - log_block[..., None])
        grad_values = grad_values + jnp.einsum(
            "hqk,qhd->khd",
            probs_full.astype(jnp.bfloat16),
            grad_block,
            preferred_element_type=jnp.float32,
        )
        grad_weights = jnp.einsum(
            "qhd,khd->hqk", grad_block, values, preferred_element_type=jnp.float32
        )
        centre = jnp.sum(probs_full * grad_weights, axis=-1, keepdims=True)
        grad_scores = (probs_full * (grad_weights - centre)).astype(jnp.bfloat16)
        grad_query = (
            jnp.einsum("hqk,khd->qhd", grad_scores, keys, preferred_element_type=jnp.float32)
            * factor
        )
        grad_keys = (
            grad_keys
            + jnp.einsum(
                "hqk,qhd->khd", grad_scores, query_block, preferred_element_type=jnp.float32
            )
            * factor
        )
        return ((grad_keys, grad_values), grad_query)

    zeros = jnp.zeros((length, local_heads, head_size), jnp.float32)
    block_in = (
        queries.reshape(block_count, block_len, local_heads, head_size),
        picture.reshape(block_count, block_len),
        places.reshape(block_count, block_len),
        grad_mixed.reshape(block_count, block_len, local_heads, head_size),
        log_total,
    )
    (grad_keys, grad_values), grad_queries = lax.scan(one_block, (zeros, zeros), block_in)
    return (grad_queries.reshape(length, local_heads, head_size), grad_keys, grad_values)


def rows_term(left, right):
    return lax.dot_general(
        left, right, (((0,), (0,)), ((), ())), preferred_element_type=jnp.float32
    )


def contract_back(grad_out, weight):
    return lax.dot_general(
        grad_out, weight, (((1,), (1,)), ((), ())), preferred_element_type=jnp.float32
    )


def shards(
    tokens,
    picture_ids,
    patch_rows,
    patch_cols,
    norm1_gain,
    norm1_bias,
    qkv_weight,
    qkv_bias,
    proj_weight,
    proj_bias,
    norm2_gain,
    norm2_bias,
    fc1_weight,
    fc1_bias,
    fc2_weight,
    fc2_bias,
    cotangent,
):
    seq_devices = lax.axis_size("seq")
    row_count, shard_len, model_width = tokens.shape
    flat_rows = row_count * shard_len
    head_size = HD
    head_count = model_width // head_size
    local_heads = head_count // seq_devices
    attn_params = (
        lax.all_gather(norm1_gain, "fsdp", axis=0, tiled=True),
        lax.all_gather(norm1_bias, "fsdp", axis=0, tiled=True),
        lax.all_gather(qkv_weight, "fsdp", axis=0, tiled=True),
        lax.all_gather(qkv_bias, "fsdp", axis=0, tiled=True),
        lax.all_gather(proj_weight, "fsdp", axis=0, tiled=True),
        lax.all_gather(proj_bias, "fsdp", axis=0, tiled=True),
    )
    mlp_params = (
        lax.all_gather(norm2_gain, "fsdp", axis=0, tiled=True),
        lax.all_gather(norm2_bias, "fsdp", axis=0, tiled=True),
        lax.all_gather(fc1_weight, "fsdp", axis=0, tiled=True),
        lax.all_gather(fc1_bias, "fsdp", axis=0, tiled=True),
        lax.all_gather(fc2_weight, "fsdp", axis=0, tiled=True),
        lax.all_gather(fc2_bias, "fsdp", axis=0, tiled=True),
    )
    picture = lax.all_gather(picture_ids, "seq", axis=1, tiled=True)
    gain_one, bias_one, weight_qkv, bias_qkv, weight_proj, bias_proj = attn_params
    gain_two, bias_two, weight_up, bias_up, weight_down, bias_down = mlp_params
    inputs = tokens.reshape(flat_rows, model_width).astype(jnp.float32)
    normed_one, factor_one = standardize(inputs)
    attn_input = (normed_one * gain_one.astype(jnp.float32) + bias_one.astype(jnp.float32)).astype(
        jnp.bfloat16
    )
    projected = (
        jnp.dot(attn_input, weight_qkv, preferred_element_type=jnp.float32)
        + bias_qkv.astype(jnp.float32)
    ).reshape(row_count, shard_len, 3, head_count, head_size)
    cosine, sine = rotary_tables(patch_rows, patch_cols, head_size)
    packed = jnp.stack(
        [
            rotate(projected[:, :, 0], cosine, sine),
            rotate(projected[:, :, 1], cosine, sine),
            projected[:, :, 2],
        ],
        axis=2,
    )
    packed = packed.astype(jnp.bfloat16).reshape(row_count, shard_len, 3, model_width)
    regrouped = lax.all_to_all(packed, "seq", split_axis=3, concat_axis=1, tiled=True)
    length = regrouped.shape[1]
    regrouped = regrouped.reshape(row_count, length, 3, local_heads, head_size)
    queries = regrouped[:, :, 0]
    keys = regrouped[:, :, 1]
    values = regrouped[:, :, 2]
    mixed, log_total = lax.map(attend_row, (queries, keys, values, picture))
    mixed_low = mixed.astype(jnp.bfloat16).reshape(row_count, length, local_heads * head_size)
    gathered = lax.all_to_all(mixed_low, "seq", split_axis=1, concat_axis=2, tiled=True).reshape(
        flat_rows, model_width
    )
    middle = (
        inputs
        + jnp.dot(gathered, weight_proj, preferred_element_type=jnp.float32)
        + bias_proj.astype(jnp.float32)
    )
    normed_two, factor_two = standardize(middle)
    mlp_input = (normed_two * gain_two.astype(jnp.float32) + bias_two.astype(jnp.float32)).astype(
        jnp.bfloat16
    )
    before = jnp.dot(mlp_input, weight_up, preferred_element_type=jnp.float32) + bias_up.astype(
        jnp.float32
    )
    gate_sig = jax.nn.sigmoid(1.702 * before)
    activated = (before * gate_sig).astype(jnp.bfloat16)
    block_out = (
        middle
        + jnp.dot(activated, weight_down, preferred_element_type=jnp.float32)
        + bias_down.astype(jnp.float32)
    ).astype(jnp.bfloat16)
    back_attn = (
        lax.all_gather(norm1_gain, "fsdp", axis=0, tiled=True),
        lax.all_gather(norm1_bias, "fsdp", axis=0, tiled=True),
        lax.all_gather(qkv_weight, "fsdp", axis=0, tiled=True),
        lax.all_gather(qkv_bias, "fsdp", axis=0, tiled=True),
        lax.all_gather(proj_weight, "fsdp", axis=0, tiled=True),
        lax.all_gather(proj_bias, "fsdp", axis=0, tiled=True),
    )
    back_mlp = (
        lax.all_gather(norm2_gain, "fsdp", axis=0, tiled=True),
        lax.all_gather(norm2_bias, "fsdp", axis=0, tiled=True),
        lax.all_gather(fc1_weight, "fsdp", axis=0, tiled=True),
        lax.all_gather(fc1_bias, "fsdp", axis=0, tiled=True),
        lax.all_gather(fc2_weight, "fsdp", axis=0, tiled=True),
        lax.all_gather(fc2_bias, "fsdp", axis=0, tiled=True),
    )
    upstream = cotangent.reshape(flat_rows, model_width)
    grad_down = lax.psum_scatter(
        rows_term(activated, upstream).astype(jnp.bfloat16), "fsdp", scatter_dimension=0, tiled=True
    )
    grad_activated = contract_back(upstream, back_mlp[4])
    grad_before = (
        grad_activated * (gate_sig + 1.702 * before * gate_sig * (1.0 - gate_sig))
    ).astype(jnp.bfloat16)
    grad_up = lax.psum_scatter(
        rows_term(mlp_input, grad_before).astype(jnp.bfloat16),
        "fsdp",
        scatter_dimension=0,
        tiled=True,
    )
    grad_mlp_input = contract_back(grad_before, back_mlp[2])
    grad_middle = upstream.astype(jnp.float32) + norm_back(
        grad_mlp_input, normed_two, factor_two, back_mlp[0].astype(jnp.float32)
    )
    grad_branch = grad_middle.astype(jnp.bfloat16)
    grad_mixed = (
        contract_back(grad_branch, back_attn[4])
        .astype(jnp.bfloat16)
        .reshape(row_count, shard_len, model_width)
    )
    grad_heads = lax.all_to_all(grad_mixed, "seq", split_axis=2, concat_axis=1, tiled=True).reshape(
        row_count, length, local_heads, head_size
    )
    grad_queries, grad_keys, grad_values = lax.map(
        attend_back, (queries, keys, values, picture, grad_heads, log_total)
    )
    stacked = (
        jnp.stack([grad_queries, grad_keys, grad_values], axis=2)
        .astype(jnp.bfloat16)
        .reshape(row_count, length, 3, local_heads * head_size)
    )
    returned = (
        lax.all_to_all(stacked, "seq", split_axis=1, concat_axis=3, tiled=True)
        .astype(jnp.float32)
        .reshape(row_count, shard_len, 3, head_count, head_size)
    )
    grad_projected = jnp.stack(
        [
            unrotate(returned[:, :, 0], cosine, sine),
            unrotate(returned[:, :, 1], cosine, sine),
            returned[:, :, 2],
        ],
        axis=2,
    )
    grad_projected = grad_projected.reshape(flat_rows, 3 * model_width).astype(jnp.bfloat16)
    grad_qkv = lax.psum_scatter(
        rows_term(attn_input, grad_projected).astype(jnp.bfloat16),
        "fsdp",
        scatter_dimension=0,
        tiled=True,
    )
    grad_attn_input = contract_back(grad_projected, back_attn[2])
    tokens_grad = grad_middle + norm_back(
        grad_attn_input, normed_one, factor_one, back_attn[0].astype(jnp.float32)
    )
    proj_full = lax.dot_general(
        gathered, grad_branch, (((0,), (0,)), ((), ())), preferred_element_type=jnp.float32
    )
    others = (
        lax.psum_scatter(
            proj_full.astype(jnp.bfloat16), "fsdp", scatter_dimension=0, tiled=True
        ).astype(jnp.float32),
        lax.psum_scatter(
            jnp.sum(grad_branch.astype(jnp.float32), axis=0).astype(jnp.bfloat16),
            "fsdp",
            scatter_dimension=0,
            tiled=True,
        ).astype(jnp.float32),
        lax.psum_scatter(
            jnp.sum(grad_attn_input * normed_one, axis=0).astype(jnp.bfloat16),
            "fsdp",
            scatter_dimension=0,
            tiled=True,
        ).astype(jnp.float32),
        lax.psum_scatter(
            jnp.sum(grad_attn_input, axis=0).astype(jnp.bfloat16),
            "fsdp",
            scatter_dimension=0,
            tiled=True,
        ).astype(jnp.float32),
        lax.psum_scatter(
            jnp.sum(grad_projected.astype(jnp.float32), axis=0).astype(jnp.bfloat16),
            "fsdp",
            scatter_dimension=0,
            tiled=True,
        ).astype(jnp.float32),
        lax.psum_scatter(
            jnp.sum(grad_mlp_input * normed_two, axis=0).astype(jnp.bfloat16),
            "fsdp",
            scatter_dimension=0,
            tiled=True,
        ).astype(jnp.float32),
        lax.psum_scatter(
            jnp.sum(grad_mlp_input, axis=0).astype(jnp.bfloat16),
            "fsdp",
            scatter_dimension=0,
            tiled=True,
        ).astype(jnp.float32),
        lax.psum_scatter(
            jnp.sum(grad_before.astype(jnp.float32), axis=0).astype(jnp.bfloat16),
            "fsdp",
            scatter_dimension=0,
            tiled=True,
        ).astype(jnp.float32),
        lax.psum_scatter(
            jnp.sum(upstream.astype(jnp.float32), axis=0).astype(jnp.bfloat16),
            "fsdp",
            scatter_dimension=0,
            tiled=True,
        ).astype(jnp.float32),
    )
    summed = (
        lax.psum(others[2].astype(jnp.bfloat16), "seq").astype(jnp.float32),
        lax.psum(others[3].astype(jnp.bfloat16), "seq").astype(jnp.float32),
        lax.psum(grad_qkv, "seq").astype(jnp.float32),
        lax.psum(others[4].astype(jnp.bfloat16), "seq").astype(jnp.float32),
        lax.psum(others[0].astype(jnp.bfloat16), "seq").astype(jnp.float32),
        lax.psum(others[1].astype(jnp.bfloat16), "seq").astype(jnp.float32),
        lax.psum(others[5].astype(jnp.bfloat16), "seq").astype(jnp.float32),
        lax.psum(others[6].astype(jnp.bfloat16), "seq").astype(jnp.float32),
        lax.psum(grad_up, "seq").astype(jnp.float32),
        lax.psum(others[7].astype(jnp.bfloat16), "seq").astype(jnp.float32),
        lax.psum(grad_down, "seq").astype(jnp.float32),
        lax.psum(others[8].astype(jnp.bfloat16), "seq").astype(jnp.float32),
    )
    return (
        block_out.reshape(row_count, shard_len, model_width),
        tokens_grad.reshape(row_count, shard_len, model_width),
        summed[0],
        summed[1],
        summed[2],
        summed[3],
        summed[4],
        summed[5],
        summed[6],
        summed[7],
        summed[8],
        summed[9],
        summed[10],
        summed[11],
    )


def solution(mesh):
    in_specs = (
        P("fsdp", "seq", None),
        P("fsdp", "seq"),
        P("fsdp", "seq"),
        P("fsdp", "seq"),
        P("fsdp"),
        P("fsdp"),
        P("fsdp", None),
        P("fsdp"),
        P("fsdp", None),
        P("fsdp"),
        P("fsdp"),
        P("fsdp"),
        P("fsdp", None),
        P("fsdp"),
        P("fsdp", None),
        P("fsdp"),
        P("fsdp", "seq", None),
    )
    out_specs = (
        P("fsdp", "seq", None),
        P("fsdp", "seq", None),
        P("fsdp"),
        P("fsdp"),
        P("fsdp", None),
        P("fsdp"),
        P("fsdp", None),
        P("fsdp"),
        P("fsdp"),
        P("fsdp"),
        P("fsdp", None),
        P("fsdp"),
        P("fsdp", None),
        P("fsdp"),
    )
    return jax.shard_map(shards, mesh=mesh, in_specs=in_specs, out_specs=out_specs, check_vma=False)
```

profile of v0, /device:TPU:16, one launch (start us, length us, event | category | flops | bytes accessed | tf_op | source)
XLA Modules:
  0.0 1063.0 jit_solution(18437321899699914661)
XLA Ops:
  13.5 24.3 %all-reduce.16 = (bf16[3840]{0:T(1024)(128)(2,1)S(1)}, bf16[1280]{0:T(1024)(128)(2,1)S(1)}, bf16[1280]{0:T(1024)(128)(2,1)S(1)}, bf16[1280]{0:T(1024)(128)(2,1)S...) all-reduce(bf16[3840]{0:T(1024)(128)(2,1)S(1)} %dynamic-update-slic, ...), channel_id=1, replica_groups=mesh['seq'=4,'fsdp'=8] {'fsdp'}, use_global_device_ids=true, to_apply=%add.2 | all-reduce | flops 10240 | bytes 40960
  38.9 64.4 %all-gather.6.cloned.1.call-done = bf16[1280,3840]{1,0:T(8,128)(2,1)} async-done(((bf16[160,3840]{1,0:T(8,128)(2,1)}), bf16[1280,3840]{1,0:T(8,128)(2,1)}) %all-gather.6.cloned.1.call-update) | async-done | bytes 9830416 | tf_op jit(solution)/shard_map/all_gather | solution.py:184
  103.4 8.7 convolution_add_fusion.1
  112.0 5.5 copy.85
  123.7 11.2 %copy.86 = bf16[1,256,3,1280]{1,2,0,3:T(4,128)(2,1)} copy(bf16[1,256,3,1280]{1,3,2,0:T(8,128)(2,1)S(1)} %pad_maximum_fusion) | data formatting | bytes 3932160 | tf_op jit(solution)/shard_map/stack | solution.py:210
  134.8 3.8 all-to-all-start
  138.7 32.7 %all_gather.45 = s32[1,1024]{1,0:T(1,128)S(1)} all-gather(s32[1,256]{1,0:T(1,128)S(1)} %copy-done.47), channel_id=1, replica_groups=mesh['seq'=4,'fsdp'=8] {'seq'}, dimensions={1}, use_global_device_ids=true | all-gather | bytes 5120 | tf_op jit(solution)/shard_map/all_gather | solution.py:197
  179.8 16.2 %while.47 = (s32[]{:T(128)}, bf16[2,512,4,80]{1,3,2,0:T(8,128)(2,1)S(1)}, f32[2,4,512]{2,1,0:T(4,128)S(1)}, s32[2,512]{1,0:T(2,128)S(1)}, s32[1024]{0:T(1024)S(1...) while((s32[]{:T(128)}, ...), condition=%wide.region_5.6_spmd, body=%wide.region_2.5_spmd.sunk | while | flops 698350592 | bytes 29644924 | solution.py:91
  184.8 3.1 fusion.146
  192.9 3.1 fusion.146
  197.5 6.4 reshape.965
  204.4 6.6 reduce.11
  212.8 4.4 all-to-all-start.1
  217.2 14.4 %all-gather = bf16[8,1,640]{2,1,0:T(2,128)(2,1)S(1)} all-gather(bf16[1,1,640]{2,1,0:T(2,128)(2,1)S(1)} %reshape.948), channel_id=1, replica_groups=mesh['seq'=4,'fsdp'=8] {'fsdp'}, dimensions={0}, use_global_device_ids=true | all-gather | bytes 11520 | tf_op jit(solution)/shard_map/all_gather | solution.py:193
  239.1 3.4 fusion.98
  242.7 21.6 %all-gather.10.cloned.1.call-done = bf16[1280,5120]{1,0:T(8,128)(2,1)} async-done(((bf16[160,5120]{1,0:T(8,128)(2,1)}), bf16[1280,5120]{1,0:T(8,128)(2,1)}) %all-gather.10.cloned.1.call-update) | async-done | bytes 13107216 | tf_op jit(solution)/shard_map/all_gather | solution.py:192
  264.3 10.3 convolution_add_fusion
  274.7 110.4 %all-gather.12.cloned.1.call-done = bf16[5120,1280]{1,0:T(8,128)(2,1)} async-done(((bf16[640,1280]{1,0:T(8,128)(2,1)}), bf16[5120,1280]{1,0:T(8,128)(2,1)}) %all-gather.12.cloned.1.call-update) | async-done | bytes 13107216 | tf_op jit(solution)/shard_map/all_gather | solution.py:194
  385.0 16.0 %fusion.99 = (bf16[5120]{0:T(1024)(128)(2,1)}, bf16[256,5120]{1,0:T(8,128)(2,1)}) fusion(f32[256,5120]{1,0:T(8,128)} %convolution_add_fusion, bf16[5120,1280]{1,0:T(8,128)(2,1)} %all-gather.12.cloned.1.call-done, bf16[1,256,1280]{2,1,0:T(8,128)(2,1)S(1)} %copy-done.16), kind=kOutput, calls=%fused_computation.169 | convolution fusion | flops 3369856000 | bytes 21637120 | tf_op jit(solution)/shard_map/dot_general | solution.py:151
  401.0 9.1 multiply_reduce_fusion.1
  415.1 8.2 reduce.12
  426.0 4.2 all-to-all-start.2
  430.3 4.0 convolution_convert_fusion.3
  434.4 6.0 all-to-all-done.2
  440.4 3.7 reshape.990
  450.1 38.7 %while.48 = (s32[]{:T(128)}, f32[1024,4,80]{0,2,1:T(8,128)S(1)}, f32[1024,4,80]{0,2,1:T(8,128)}, bf16[2,512,4,80]{1,3,2,0:T(8,128)(2,1)}, bf16[2,512,4,80]{1,3,2...) while((s32[]{:T(128)}, f32[1024,4,80]{0,2,1:T(8,128)S(1)}, ...), condition=%wide.region_12.13_spmd.clone, body=%wide.region_10.12_spmd.clone.sunk | while | flops 1713077248 | bytes 181746144 | solution.py:140
  452.2 3.2 multiply_reduce_fusion.7
  455.4 3.7 multiply_convert_fusion.5
  459.2 3.4 fusion.158
  471.5 3.2 multiply_reduce_fusion.7
  474.8 3.7 multiply_convert_fusion.5
  478.5 3.3 fusion.158
  493.9 4.8 copy.99
  498.7 39.7 %all_to_all.54 = bf16[1,1024,3,320]{3,2,0,1:T(4,128)(2,1)} all-to-all(bf16[1,1024,3,320]{3,2,0,1:T(4,128)(2,1)S(1)} %copy.99), channel_id=1, replica_groups=mesh['seq'=4,'fsdp'=8] {'seq'}, dimensions={1} | all-to-all | bytes 3932160 | tf_op jit(solution)/shard_map/all_to_all | solution.py:301
  538.4 4.4 copy.100
  542.8 3.3 reshape.926
  553.0 5.6 convolution_convert_fusion.2
  560.0 8.6 convolution_convert_fusion.1
  569.7 11.5 %convolution_convert_fusion = bf16[5120,1280]{1,0:T(8,128)(2,1)} fusion(bf16[1,256,1280]{2,1,0:T(8,128)(2,1)S(1)} %copy-done.17, f32[256,5120]{1,0:T(8,128)} %convolution_add_fusion), kind=kOutput, calls=%fused_computation.58 | convolution fusion | flops 3369861120 | bytes 19005440 | tf_op jit(solution)/shard_map/dot_general | solution.py:145
  581.3 76.8 %reduce-scatter.5.cloned.1.call-done = bf16[160,3840]{1,0:T(8,128)(2,1)} async-done(((bf16[1280,3840]{1,0:T(8,128)(2,1)}), bf16[160,3840]{1,0:T(8,128)(2,1)}) %reduce-scatter.5.cloned.1.call-update) | async-done | bytes 1228816 | tf_op jit(solution)/shard_map/reduce_scatter | solution.py:314
  658.1 134.9 %reduce-scatter.9.cloned.1.call-done = bf16[160,5120]{1,0:T(8,128)(2,1)} async-done(((bf16[1280,5120]{1,0:T(8,128)(2,1)}), bf16[160,5120]{1,0:T(8,128)(2,1)}) %reduce-scatter.9.cloned.1.call-update) | async-done | bytes 1638416 | tf_op jit(solution)/shard_map/reduce_scatter | solution.py:273
  793.0 134.9 %reduce-scatter.11.cloned.1.call-done = bf16[640,1280]{1,0:T(8,128)(2,1)} async-done(((bf16[5120,1280]{1,0:T(8,128)(2,1)}), bf16[640,1280]{1,0:T(8,128)(2,1)}) %reduce-scatter.11.cloned.1.call-update) | async-done | bytes 1638416 | tf_op jit(solution)/shard_map/reduce_scatter | solution.py:266
  930.4 8.5 fusion.65
  938.9 23.1 %all-reduce.15 = (bf16[1280]{0:T(1024)(128)(2,1)S(1)}, bf16[1280]{0:T(1024)(128)(2,1)S(1)}, bf16[1280]{0:T(1024)(128)(2,1)S(1)}, bf16[3840]{0:T(1024)(128)(2,1)S...) all-reduce(bf16[1280]{0:T(1024)(128)(2,1)S(1)} %dynamic-update-slic, ...), channel_id=1, replica_groups=mesh['seq'=4,'fsdp'=8] {'fsdp'}, use_global_device_ids=true, to_apply=%add.6 | all-reduce | flops 17920 | bytes 71680
  962.6 10.3 all-reduce.17
  980.4 11.5 %fusion.49 = bf16[1,256,1280]{2,1,0:T(8,128)(2,1)} fusion(f32[256,1280]{1,0:T(8,128)S(1)} %copy-done.7, bf16[5120,1280]{1,0:T(8,128)(2,1)} %all-gather.12.cloned.1.call-done, f32[1280]{0:T(1024)S(1)} %convert_element_type.255, f32[256,5120]{1,0:T(8,128)} %convolution_add_fusion), kind=kOutput, calls=%fused_computation.75 | convolution fusion | flops 3364290560 | bytes 20321280 | tf_op jit(solution)/shard_map/dot_general | solution.py:246
  991.8 56.3 %all-reduce.21.cloned.1.call-done = (bf16[160,3840]{1,0:T(8,128)(2,1)}, bf16[160,1280]{1,0:T(8,128)(2,1)}, bf16[160,5120]{1,0:T(8,128)(2,1)}, bf16[640,1280]{1,0:T(8,128)(2,1)}) async-done(((bf16[160,3840]{1,0:T(8,128)(2,1)}, bf16[160,1280]{1,0:T(8,128)(2,1)}, bf16[160,5120]{1,0:T(8,128)(2,1)}, bf16[640,1280]{1,0:T(8,128)(2,1)}), (bf16[160,3840]{1,0:T(8,128)(2,1)}, bf16[160,1280]{1,0:T(8,128)(2,1)}, ...) | async-done | bytes 4915216 | tf_op jit(solution)/shard_map/psum | solution.py:383
  1048.1 3.0 convert_element_type.274
  (292 shorter events, 100.8 us)
Async XLA Ops:
  7.2 96.2 %all-gather.6.cloned.1.call-start = ((), (), s32[]{:S(2)}) async-start(), calls=%async_computation.8 | async-start | bytes 11059200 | tf_op jit(solution)/shard_map/all_gather | solution.py:184
  7.9 4.1 copy-start.52
  7.9 4.3 copy-start.53
  7.9 4.6 copy-start.54
  8.0 4.8 copy-start.55
  8.0 5.1 copy-start.56
  8.0 5.3 copy-start.48
  8.0 29.9 %copy-start.49 = (s32[1,256]{1,0:T(1,128)S(1)}, s32[1,256]{1,0:T(1,128)}, u32[]{:S(2)}) copy-start(s32[1,256]{1,0:T(1,128)} %param.23) | copy-start | bytes 3076
  8.0 29.9 %copy-start.50 = (s32[1,256]{1,0:T(1,128)S(1)}, s32[1,256]{1,0:T(1,128)}, u32[]{:S(2)}) copy-start(s32[1,256]{1,0:T(1,128)} %param.24) | copy-start | bytes 3076
  8.0 30.3 %copy-start.8 = (bf16[1,256,1280]{2,1,0:T(8,128)(2,1)S(1)}, bf16[1,256,1280]{2,1,0:T(8,128)(2,1)}, u32[]{:S(2)}) copy-start(bf16[1,256,1280]{2,1,0:T(8,128)(2,1)} %param.21) | copy-start | bytes 1966084
  8.0 231.0 %all-gather.8.cloned.1.call-start = ((), (), s32[]{:S(2)}) async-start(), calls=%async_computation.9 | async-start | bytes 3686400 | tf_op jit(solution)/shard_map/all_gather | solution.py:186
  8.8 255.6 %all-gather.10.cloned.1.call-start = ((), (), s32[]{:S(2)}) async-start(), calls=%async_computation.10 | async-start | bytes 14745600 | tf_op jit(solution)/shard_map/all_gather | solution.py:192
  9.5 375.5 %all-gather.12.cloned.1.call-start = ((), (), s32[]{:S(2)}) async-start(), calls=%async_computation.11 | async-start | bytes 14745600 | tf_op jit(solution)/shard_map/all_gather | solution.py:194
  37.9 74.1 %copy-start.33 = (f32[1280]{0:T(1024)}, f32[1280]{0:T(1024)S(1)}, u32[]{:S(2)}) copy-start(f32[1280]{0:T(1024)S(1)} %convert_element_type.242) | copy-start | bytes 15364
  37.9 74.1 %copy-start.31 = (f32[1280]{0:T(1024)}, f32[1280]{0:T(1024)S(1)}, u32[]{:S(2)}) copy-start(f32[1280]{0:T(1024)S(1)} %convert_element_type.241) | copy-start | bytes 15364
  38.4 82.8 %copy-start.26 = (f32[256,80]{0,1:T(8,128)}, f32[256,80]{0,1:T(8,128)S(1)}, u32[]{:S(2)}) copy-start(f32[256,80]{0,1:T(8,128)S(1)} %get-tuple-element.435) | copy-start | bytes 245764
  38.4 82.8 %copy-start.28 = (f32[256,80]{0,1:T(8,128)}, f32[256,80]{0,1:T(8,128)S(1)}, u32[]{:S(2)}) copy-start(f32[256,80]{0,1:T(8,128)S(1)} %get-tuple-element.436) | copy-start | bytes 245764
  38.6 73.5 %copy-start.37 = (f32[256]{0:T(256)}, f32[256]{0:T(256)S(1)}, u32[]{:S(2)}) copy-start(f32[256]{0:T(256)S(1)} %broadcast_multiply_fusion.7) | copy-start | bytes 3076
  38.9 73.1 %copy-start.40 = (f32[256]{0:T(256)}, f32[256]{0:T(256)S(1)}, u32[]{:S(2)}) copy-start(f32[256]{0:T(256)S(1)} %add_rsqrt_fusion.1) | copy-start | bytes 3076
  134.8 3.9 copy-start.47
  134.8 37.8 %all-to-all-start = ((bf16[1,256,3,1280]{1,2,0,3:T(4,128)(2,1)}), bf16[1,256,3,1280]{1,2,0,3:T(4,128)(2,1)S(1)}, u32[]{:S(2)}, u32[]{:S(2)}) async-start(bf16[1,256,3,1280]{1,2,0,3:T(4,128)(2,1)} %copy.86), calls=%async_computation | async-start | bytes 5242880 | tf_op jit(solution)/shard_map/all_to_all | solution.py:219
  196.0 7.9 copy-start.4
  211.0 6.2 copy-start.46
  212.8 18.9 %all-to-all-start.1 = ((bf16[4,2,40960]{2,1,0:T(2,128)(2,1)}), bf16[4,2,40960]{2,1,0:T(2,128)(2,1)S(1)}, u32[]{:S(2)}, u32[]{:S(2)}) async-start(bf16[4,2,40960]{2,1,0:T(2,128)(2,1)} %reshape.987), calls=%async_computation.1 | async-start | bytes 1310720 | tf_op jit(solution)/shard_map/all_to_all | solution.py:227
  231.7 32.6 %copy-start.35 = (f32[1280]{0:T(1024)}, f32[1280]{0:T(1024)S(1)}, u32[]{:S(2)}) copy-start(f32[1280]{0:T(1024)S(1)} %convert_element_type.251) | copy-start | bytes 15364
  242.4 167.7 %copy-start.6 = (f32[256,1280]{1,0:T(8,128)}, f32[256,1280]{1,0:T(8,128)S(1)}, u32[]{:S(2)}) copy-start(f32[256,1280]{1,0:T(8,128)S(1)} %get-tuple-element.442) | copy-start | bytes 3932164
  264.3 120.7 %copy-start.16 = (bf16[1,256,1280]{2,1,0:T(8,128)(2,1)S(1)}, bf16[1,256,1280]{2,1,0:T(8,128)(2,1)}, u32[]{:S(2)}) copy-start(bf16[1,256,1280]{2,1,0:T(8,128)(2,1)} %param.37) | copy-start | bytes 1966084
  415.1 15.1 %copy-start.15 = (bf16[1,256,4,320]{1,3,2,0:T(8,128)(2,1)S(1)}, bf16[1,256,4,320]{1,3,2,0:T(8,128)(2,1)}, u32[]{:S(2)}) copy-start(bf16[1,256,4,320]{1,3,2,0:T(8,128)(2,1)} %copy.93) | copy-start | bytes 1966084
  426.0 14.4 %all-to-all-start.2 = ((bf16[4,2,40960]{2,1,0:T(2,128)(2,1)}), bf16[4,2,40960]{2,1,0:T(2,128)(2,1)}, u32[]{:S(2)}, u32[]{:S(2)}) async-start(bf16[4,2,40960]{2,1,0:T(2,128)(2,1)} %reshape.989), calls=%async_computation.2 | async-start | bytes 1310720 | tf_op jit(solution)/shard_map/all_to_all | solution.py:289
  430.2 151.1 %reduce-scatter.7.cloned.1.call-start = ((), (), s32[]{:S(2)}) async-start(), calls=%async_computation.13 | async-start | bytes 3686400 | tf_op jit(solution)/shard_map/reduce_scatter | solution.py:328
  434.3 223.7 %reduce-scatter.5.cloned.1.call-start = ((), (), s32[]{:S(2)}) async-start(), calls=%async_computation.12 | async-start | bytes 11059200 | tf_op jit(solution)/shard_map/reduce_scatter | solution.py:314
  451.4 4.0 copy-start
  459.2 4.8 copy-start.1
  459.2 4.9 copy-start.13
  459.2 5.3 copy-start.24
  470.8 4.0 copy-start
  478.5 4.6 copy-start.1
  478.5 4.7 copy-start.13
  478.5 5.1 copy-start.24
  558.7 234.3 %reduce-scatter.9.cloned.1.call-start = ((), (), s32[]{:S(2)}) async-start(), calls=%async_computation.14 | async-start | bytes 14745600 | tf_op jit(solution)/shard_map/reduce_scatter | solution.py:273
  568.6 359.2 %reduce-scatter.11.cloned.1.call-start = ((), (), s32[]{:S(2)}) async-start(), calls=%async_computation.15 | async-start | bytes 14745600 | tf_op jit(solution)/shard_map/reduce_scatter | solution.py:266
  581.2 466.9 %all-reduce.21.cloned.1.call-start = ((), (), s32[]{:S(2)}) async-start(), calls=%async_computation.16 | async-start | bytes 9830400 | tf_op jit(solution)/shard_map/psum | solution.py:383
  930.3 8.6 copy-start.39
  930.3 8.6 copy-start.42
  930.3 8.6 copy-start.43
  930.3 8.6 copy-start.44
  930.3 47.2 %copy-start.11 = (f32[256,1280]{1,0:T(8,128)S(1)}, f32[256,1280]{1,0:T(8,128)}, u32[]{:S(2)}) copy-start(f32[256,1280]{1,0:T(8,128)} %copy-done.10) | copy-start | bytes 3932164
  1048.1 4.0 copy-start.23
  (32 other events, 61.8 us)
Sparse Core Ops, SparseCore 0:
  9.6 93.6 all-gather.5
  105.0 38.2 all-gather.7
  144.9 119.3 all-gather.9
  265.8 119.1 all-gather.11
  434.5 38.6 reduce-scatter.6
  558.8 99.2 reduce-scatter.4
  660.4 132.5 reduce-scatter.8
  795.3 132.5 reduce-scatter.10
  931.7 116.3 all-reduce.20
where the time goes:
time: 1080 us; the launch traced here: 1060 us
  waiting for transfers between devices  608 us (56%)
  blocking collectives  145 us (13%)
  matrix products  132 us (12%)
  local copies, waits for them, and re-layouts  91.9 us (9%)
  other arithmetic  54.9 us (5%)
  between operations  18.4 us (2%)
  starting transfers between devices  12.7 us (1%)
    reduce_scatter x1, waiting for transfers between devices, shards(): lax.psum_scatter(rows_term(mlp_input, grad_before).astype(jnp.bfloat16),...  135 us
    reduce_scatter x1, waiting for transfers between devices, shards(): lax.psum_scatter(rows_term(activated, upstream).astype(jnp.bfloat16), 'fs...  135 us
    all_gather x1, waiting for transfers between devices, shards(): lax.all_gather(fc2_weight, 'fsdp', axis=0, tiled=True)  110 us
    reduce_scatter x1, waiting for transfers between devices, shards(): lax.psum_scatter(rows_term(attn_input, grad_projected).astype(jnp.bfloat1...  76.8 us
    all_gather x1, waiting for transfers between devices, shards(): lax.all_gather(qkv_weight, 'fsdp', axis=0, tiled=True)  64.4 us
    psum x1, waiting for transfers between devices, shards(): lax.psum(grad_qkv, 'seq').astype(jnp.float32)  56.3 us
    unnamed x2, blocking collectives  47.4 us
    all_to_all x1, blocking collectives, shards(): lax.all_to_all(stacked, 'seq', split_axis=1, concat_axis=3, tiled=True)  39.7 us
  transfers between devices with their start and end apart: 12, of which 8 were waited for; matrix products, arithmetic and copies ran while one was open for 21% of the time, Pallas kernels for 0%

commit v1 on v0

v1 whole, which is shorter than its diff:
```python
import jax
import jax.numpy as jnp
from jax import lax
from jax.sharding import PartitionSpec as P

HD = 80
NORM_EPSILON = 1e-06
MASKED = -1e30
BF = jnp.bfloat16
F32 = jnp.float32


def standardize(values_in):
    centre = jnp.mean(values_in, axis=-1, keepdims=True)
    shifted = values_in - centre
    factor = lax.rsqrt(jnp.mean(shifted * shifted, axis=-1, keepdims=True) + NORM_EPSILON)
    return (shifted * factor, factor)


def norm_back(grad_out, normed, factor, gain):
    scaled = grad_out * gain
    return factor * (
        scaled
        - jnp.mean(scaled, axis=-1, keepdims=True)
        - normed * jnp.mean(scaled * normed, axis=-1, keepdims=True)
    )


def rotary_tables(patch_row, patch_col, head_size):
    quarter = head_size // 4
    inverse = jnp.power(10000.0, -jnp.arange(quarter, dtype=F32) / quarter)
    half_angles = jnp.concatenate(
        [
            patch_row.astype(F32)[..., None] * inverse,
            patch_col.astype(F32)[..., None] * inverse,
        ],
        axis=-1,
    )
    angles = jnp.concatenate([half_angles, half_angles], axis=-1)
    return (jnp.cos(angles)[..., None, :], jnp.sin(angles)[..., None, :])


def rotate(values_in, cosine, sine):
    half_size = values_in.shape[-1] // 2
    turned = jnp.concatenate([-values_in[..., half_size:], values_in[..., :half_size]], axis=-1)
    return values_in * cosine + turned * sine


def unrotate(grad_in, cosine, sine):
    half_size = grad_in.shape[-1] // 2
    moved = grad_in * sine
    return grad_in * cosine + jnp.concatenate(
        [moved[..., half_size:], -moved[..., :half_size]], axis=-1
    )


def masked_scores(queries, keys, picture, factor):
    places = jnp.arange(picture.shape[0], dtype=jnp.int32)
    scores = jnp.einsum("qhd,khd->hqk", queries, keys, preferred_element_type=F32) * factor
    allowed = (picture[:, None] == picture[None, :]) & (
        (picture[None, :] >= 0) | (places[:, None] == places[None, :])
    )
    return jnp.where(allowed[None, :, :], scores, MASKED)


def attend(queries, keys, values, picture):
    scores = masked_scores(queries, keys, picture, HD**-0.5)
    row_max = jnp.max(scores, axis=-1, keepdims=True)
    powers = jnp.exp(scores - row_max)
    totals = jnp.sum(powers, axis=-1, keepdims=True)
    weights = (powers / totals).astype(BF)
    mixed = jnp.einsum("hqk,khd->qhd", weights, values, preferred_element_type=F32)
    return mixed.astype(BF), row_max + jnp.log(totals)


def attend_back(queries, keys, values, picture, grad_mixed, log_total):
    factor = HD**-0.5
    scores = masked_scores(queries, keys, picture, factor)
    probs = jnp.exp(scores - log_total)
    weights = probs.astype(BF)
    grad_values = jnp.einsum("hqk,qhd->khd", weights, grad_mixed, preferred_element_type=F32)
    grad_weights = jnp.einsum("qhd,khd->hqk", grad_mixed, values, preferred_element_type=F32)
    centre = jnp.sum(probs * grad_weights, axis=-1, keepdims=True)
    grad_scores = (probs * (grad_weights - centre)).astype(BF)
    grad_queries = jnp.einsum("hqk,khd->qhd", grad_scores, keys, preferred_element_type=F32) * factor
    grad_keys = jnp.einsum("hqk,qhd->khd", grad_scores, queries, preferred_element_type=F32) * factor
    return grad_queries.astype(BF), grad_keys.astype(BF), grad_values.astype(BF)


def dot(left, right):
    return jnp.dot(left, right, preferred_element_type=F32)


def rows_term(left, right):
    return lax.dot_general(left, right, (((0,), (0,)), ((), ())), preferred_element_type=F32)


def contract_back(grad_out, weight):
    return lax.dot_general(grad_out, weight, (((1,), (1,)), ((), ())), preferred_element_type=F32)


def gather(value, axis_name, axis=0):
    return lax.all_gather(value, axis_name, axis=axis, tiled=True)


def scatter_sum(value, axis_name, axis=0):
    return lax.psum_scatter(value, axis_name, scatter_dimension=axis, tiled=True)


def shards(
    tokens,
    picture_ids,
    patch_rows,
    patch_cols,
    norm1_gain,
    norm1_bias,
    qkv_weight,
    qkv_bias,
    proj_weight,
    proj_bias,
    norm2_gain,
    norm2_bias,
    fc1_weight,
    fc1_bias,
    fc2_weight,
    fc2_bias,
    cotangent,
):
    n = lax.axis_size("seq")
    me = lax.axis_index("seq")
    stores = lax.axis_size("fsdp")
    _, own, width = tokens.shape
    heads = width // HD
    local_heads = heads // n
    hw = local_heads * HD
    rows = qkv_weight.shape[0]
    hidden = fc1_weight.shape[1]
    part = hidden // (stores * n)

    def pick(value, axis):
        return lax.dynamic_index_in_dim(value, me, axis, keepdims=False)

    own_qkv = pick(qkv_weight.reshape(rows, 3, n, hw), 2).reshape(rows, 3 * hw)
    own_up = pick(fc1_weight.reshape(rows, stores, n, part), 2).reshape(rows, stores * part)
    own_down = pick(fc2_weight.reshape(n, part, width), 0)
    small = (norm1_gain, norm1_bias, proj_bias, norm2_gain, norm2_bias, fc2_bias, qkv_bias, fc1_bias)
    sizes = [item.shape[0] for item in small]
    packed = gather(jnp.concatenate(small)[None], "fsdp")
    weight_qkv = gather(own_qkv, "fsdp")
    weight_proj = gather(proj_weight, "fsdp")
    weight_up = gather(own_up, "fsdp")
    weight_down = gather(own_down, "fsdp")
    params = []
    start = 0
    for size in sizes:
        params.append(packed[:, start : start + size].reshape(-1).astype(F32))
        start += size
    gain_one, bias_one, bias_proj, gain_two, bias_two, bias_down, bias_qkv, bias_up = params
    bias_qkv = pick(bias_qkv.reshape(3, n, hw), 1).reshape(3 * hw)
    bias_up = pick(bias_up.reshape(stores, n, part), 1).reshape(stores * part)

    places = jnp.stack([picture_ids[0], patch_rows[0], patch_cols[0]])
    places = gather(places, "seq", 1)
    picture = places[0]
    all_tokens = gather(tokens[0], "seq").astype(F32)
    upstream = gather(cotangent[0], "seq")
    length = all_tokens.shape[0]

    def mine(value):
        return lax.dynamic_slice_in_dim(value, me * own, own, 0)

    normed_one, factor_one = standardize(all_tokens)
    attn_input = (normed_one * gain_one + bias_one).astype(BF)
    projected = (dot(attn_input, weight_qkv) + bias_qkv).reshape(length, 3, local_heads, HD)
    cosine, sine = rotary_tables(places[1], places[2], HD)
    queries = rotate(projected[:, 0], cosine, sine).astype(BF)
    keys = rotate(projected[:, 1], cosine, sine).astype(BF)
    values = projected[:, 2].astype(BF)
    mixed_own, log_total = attend(queries, keys, values, picture)
    mixed = gather(mixed_own.reshape(length, hw), "seq", 1)
    middle = all_tokens + dot(mixed, weight_proj) + bias_proj
    normed_two, factor_two = standardize(middle)
    mlp_input = (normed_two * gain_two + bias_two).astype(BF)
    before = dot(mlp_input, weight_up) + bias_up
    gate = jax.nn.sigmoid(1.702 * before)
    activated = (before * gate).astype(BF)
    out_part = dot(activated, weight_down).astype(BF)
    block_out = (mine(middle) + scatter_sum(out_part, "seq").astype(F32) + bias_down).astype(BF)

    grad_down = scatter_sum(rows_term(activated, upstream).astype(BF), "fsdp")
    grad_activated = contract_back(upstream, weight_down)
    grad_before = (grad_activated * (gate + 1.702 * before * gate * (1.0 - gate))).astype(BF)
    grad_up = scatter_sum(rows_term(mlp_input, grad_before).astype(BF), "fsdp")
    grad_mlp_input = scatter_sum(contract_back(grad_before, weight_up).astype(BF), "seq").astype(F32)
    own_upstream = cotangent[0].astype(F32)
    own_two = mine(normed_two)
    grad_middle = own_upstream + norm_back(grad_mlp_input, own_two, mine(factor_two), gain_two)
    grad_branch = grad_middle.astype(BF)
    grad_mixed = contract_back(grad_branch, weight_proj).astype(BF)
    grad_heads = lax.all_to_all(grad_mixed, "seq", split_axis=1, concat_axis=0, tiled=True)
    branch_part = lax.all_to_all(grad_branch, "seq", split_axis=1, concat_axis=0, tiled=True)
    grad_proj = scatter_sum(rows_term(mixed, branch_part).astype(BF), "fsdp")
    grad_queries, grad_keys, grad_values = attend_back(
        queries, keys, values, picture, grad_heads.reshape(length, local_heads, HD), log_total
    )
    grad_projected = jnp.stack(
        [
            unrotate(grad_queries.astype(F32), cosine, sine).astype(BF),
            unrotate(grad_keys.astype(F32), cosine, sine).astype(BF),
            grad_values,
        ],
        axis=1,
    ).reshape(length, 3 * hw)
    grad_qkv = scatter_sum(rows_term(attn_input, grad_projected).astype(BF), "fsdp")
    grad_attn_input = scatter_sum(contract_back(grad_projected, weight_qkv).astype(BF), "seq").astype(F32)
    own_one = mine(normed_one)
    tokens_grad = grad_middle + norm_back(grad_attn_input, own_one, mine(factor_one), gain_one)

    def spread(value, groups):
        empty = jnp.zeros((groups, n, value.shape[0] // groups), F32)
        return lax.dynamic_update_slice_in_dim(
            empty, value.reshape(groups, 1, -1), me, 1
        ).reshape(stores, -1)

    sums = [
        jnp.sum(grad_attn_input * own_one, axis=0).reshape(stores, -1),
        jnp.sum(grad_attn_input, axis=0).reshape(stores, -1),
        jnp.sum(grad_branch.astype(F32), axis=0).reshape(stores, -1),
        jnp.sum(grad_mlp_input * own_two, axis=0).reshape(stores, -1),
        jnp.sum(grad_mlp_input, axis=0).reshape(stores, -1),
        jnp.sum(own_upstream, axis=0).reshape(stores, -1),
        spread(jnp.sum(grad_projected.astype(F32), axis=0), 3),
        spread(jnp.sum(grad_before.astype(F32), axis=0), stores),
    ]
    summed = lax.psum(scatter_sum(jnp.concatenate(sums, axis=1), "fsdp"), "seq")[0]
    finals = []
    start = 0
    for size in sizes:
        finals.append(summed[start : start + size])
        start += size
    full_down = gather(grad_down, "seq").astype(F32)
    full_up = gather(grad_up[None], "seq").reshape(n, rows, stores, part)
    full_up = full_up.transpose(1, 2, 0, 3).reshape(rows, hidden).astype(F32)
    full_proj = gather(grad_proj, "seq", 1).astype(F32)
    full_qkv = gather(grad_qkv[None], "seq").reshape(n, rows, 3, hw)
    full_qkv = full_qkv.transpose(1, 2, 0, 3).reshape(rows, 3 * width).astype(F32)
    return (
        block_out[None],
        tokens_grad[None],
        finals[0],
        finals[1],
        full_qkv,
        finals[6],
        full_proj,
        finals[2],
        finals[3],
        finals[4],
        full_up,
        finals[7],
        full_down,
        finals[5],
    )


def solution(mesh):
    token = P("fsdp", "seq", None)
    place = P("fsdp", "seq")
    vector = P("fsdp")
    matrix = P("fsdp", None)
    in_specs = (
        token,
        place,
        place,
        place,
        vector,
        vector,
        matrix,
        vector,
        matrix,
        vector,
        vector,
        vector,
        matrix,
        vector,
        matrix,
        vector,
        token,
    )
    out_specs = (
        token,
        token,
        vector,
        vector,
        matrix,
        vector,
        matrix,
        vector,
        vector,
        vector,
        matrix,
        vector,
        matrix,
        vector,
    )
    return jax.shard_map(shards, mesh=mesh, in_specs=in_specs, out_specs=out_specs, check_vma=False)
```

time: 1080 us -> 773 us (0.72)
  waiting for transfers between devices: 608 us -> 426 us
  blocking collectives: 145 us -> 65.1 us
  matrix products: 132 us -> 119 us
  local copies, waits for them, and re-layouts: 91.9 us -> 79.3 us
    reduce_scatter x4 -> x7, waiting for transfers between devices: 347 us -> 161 us  [scatter_sum(): lax.psum_scatter(value, axis_name, scatter_dimension=axis, tiled=True)]
    psum x1 -> x0, waiting for transfers between devices: 56.3 us -> none  [shards(): lax.psum(grad_qkv, 'seq').astype(jnp.float32)]
    unnamed x9 -> x19, waiting for transfers between devices: 2.66 us -> 49.6 us
    all_gather x2, blocking collectives: 47.2 us -> 19.8 us  [gather(): return lax.all_gather(value, axis_name, axis=axis, tiled=True)]
    all_to_all x1, blocking collectives: 39.7 us -> 12.8 us  [shards(): lax.all_to_all(grad_branch, 'seq', split_axis=1, concat_axis=0, tiled=True)]
    convert_element_type x4 -> x18, local copies, waits for them, and re-layouts: 14 us -> 40.3 us  [the longest x3 21.8 us: shards(): full_up = full_up.transpose(1, 2, 0, 3).reshape(rows, hidden).astype(F32)]
    unnamed x2 -> x1, blocking collectives: 47.4 us -> 22.3 us
    all_gather x4 -> x10, waiting for transfers between devices: 196 us -> 215 us  [gather(): return lax.all_gather(value, axis_name, axis=axis, tiled=True)]
  transfers between devices with their start and end apart: 12 -> 19, of which waited for: 8 -> 15; matrix products, arithmetic and copies ran while one was open for 21% -> 28% of each run, Pallas kernels for 0% -> 0%
where the time goes in v1:
time: 773 us; the launch traced here: 766 us
  waiting for transfers between devices  426 us (55%)
  matrix products  119 us (15%)
  local copies, waits for them, and re-layouts  79.3 us (10%)
  blocking collectives  65.1 us (8%)
  other arithmetic  56.3 us (7%)
  between operations  16.1 us (2%)
    all_gather x10, waiting for transfers between devices, gather(): return lax.all_gather(value, axis_name, axis=axis, tiled=True)  215 us
    reduce_scatter x7, waiting for transfers between devices, scatter_sum(): lax.psum_scatter(value, axis_name, scatter_dimension=axis, tiled=True)  161 us
    unnamed x19, waiting for transfers between devices  49.6 us
    dot_general x4, matrix products, dot(): return jnp.dot(left, right, preferred_element_type=F32)  32.2 us
    dot_general x4, matrix products, rows_term(): lax.dot_general(left, right, (((0,), (0,)), ((), ())), preferred_element_...  28.9 us
    unnamed x1, blocking collectives  22.3 us
    convert_element_type x3, local copies, waits for them, and re-layouts, shards(): full_up = full_up.transpose(1, 2, 0, 3).reshape(rows, hidden).astype(F32)  21.8 us
    dot_general x4, matrix products, contract_back(): lax.dot_general(grad_out, weight, (((1,), (1,)), ((), ())), preferred_ele...  21.3 us
  transfers between devices with their start and end apart: 19, of which 15 were waited for; matrix products, arithmetic and copies ran while one was open for 28% of the time, Pallas kernels for 0%

profile of v1, /device:TPU:16, one launch (start us, length us, event | category | flops | bytes accessed | tf_op | source)
XLA Modules:
  0.0 766.1 jit_solution(9642049097155985330)
XLA Ops:
  17.7 8.5 %all_gather.42 = s32[3,1024]{1,0:T(4,128)S(1)} all-gather(s32[3,256]{1,0:T(4,128)S(1)} %pad_add_fusion), channel_id=1, replica_groups=mesh['seq'=4,'fsdp'=8] {'seq'}, dimensions={1}, use_global_device_ids=true | all-gather | bytes 15360 | tf_op jit(solution)/shard_map/all_gather | solution.py:103
  28.0 22.3 %all-reduce = bf16[16640]{0:T(1024)(128)(2,1)S(1)} all-reduce(bf16[16640]{0:T(1024)(128)(2,1)S(1)} %dynamic-update-slice), channel_id=3, replica_groups=mesh['seq'=4,'fsdp'=8] {'fsdp'}, use_global_device_ids=true, to_apply=%add | all-reduce | flops 16640 | bytes 66560
  58.5 27.2 %all-gather.18.cloned.1.call-done = bf16[1280,960]{1,0:T(8,128)(2,1)} async-done(((bf16[160,960]{1,0:T(8,128)(2,1)}), bf16[1280,960]{1,0:T(8,128)(2,1)}) %all-gather.18.cloned.1.call-update) | async-done | bytes 2457616 | tf_op jit(solution)/shard_map/all_gather | solution.py:103
  85.7 5.8 broadcast_add_fusion
  94.1 7.7 fusion.74
  101.8 8.1 %fusion = f32[4,1024]{1,0:T(4,128)S(1)} fusion(f32[4,1024,1024]{1,2,0:T(8,128)} %get-tuple-element.64, f32[4,1024]{1,0:T(4,128)S(1)} %get-tuple-element.63), kind=kLoop, calls=%fused_computation.6 | loop fusion | flops 8384512 | bytes 16809984 | tf_op jit(solution)/shard_map/reduce_sum | solution.py:70
  109.9 8.9 %fusion.34 = bf16[4,80,1024]{2,1,0:T(8,128)(2,1)} fusion(f32[4,1024,1024]{1,2,0:T(8,128)} %get-tuple-element.64, f32[4,1024]{1,0:T(4,128)S(1)} %fusion, f32[4,1024]{1,0:T(4,128)S(1)} %get-tuple-element.63, f32[1024,3,4,80]{0,3,2,1:T(8,128)S(1)} %bitcast.143), kind=kOutput, calls=%fused_computation.69 | convolution fusion | flops 683999232 | bytes 18120704 | tf_op jit(solution)/shard_map/hqk,khd->qhd/dot_general | solution.py:72
  118.9 5.2 reshape.440
  124.2 5.9 dynamic-slice_reduce_fusion
  133.7 33.7 %all-gather.20.cloned.1.call-done = bf16[1024,1280]{0,1:T(8,128)(2,1)} async-done(((bf16[1024,320]{0,1:T(8,128)(2,1)}), bf16[1024,1280]{0,1:T(8,128)(2,1)}) %all-gather.20.cloned.1.call-update) | async-done | bytes 2621456 | tf_op jit(solution)/shard_map/all_gather | solution.py:103
  167.4 7.7 %fusion.75 = (f32[1024]{0:T(1024)S(1)}, f32[1024,1280]{1,0:T(8,128)S(1)}) fusion(f32[1280]{0:T(1024)S(1)} %reshape.458, bf16[1024,1280]{0,1:T(8,128)(2,1)} %all-gather.20.cloned.1.call-done, bf16[1280,1280]{1,0:T(8,128)(2,1)} %all-gather.22.cloned.1.call-done, bf16[1,1024,1280]{2,1,0:T(8,128)(2,1)} %all-gather.28.cloned.1.call-done), kind=kOutput, calls=%fused_computation.150 | convolution fusion | flops 3360685056 | bytes 13771776 | tf_op jit(solution)/shard_map/dot_general | solution.py:91
  180.4 27.3 %all-gather.24.cloned.1.call-done = bf16[1280,1280]{1,0:T(8,128)(2,1)} async-done(((bf16[160,1280]{1,0:T(8,128)(2,1)}), bf16[1280,1280]{1,0:T(8,128)(2,1)}) %all-gather.24.cloned.1.call-update) | async-done | bytes 3276816 | tf_op jit(solution)/shard_map/all_gather | solution.py:103
  207.7 9.4 %fusion.55 = f32[1024,1280]{1,0:T(8,128)} fusion(bf16[1280,1280]{1,0:T(8,128)(2,1)} %all-gather.24.cloned.1.call-done, f32[1024,1280]{1,0:T(8,128)} %subtract_multiply_fusion, f32[1280]{0:T(1024)S(1)} %reshape.460, f32[1280]{0:T(1024)S(1)} %reshape.459), kind=kOutput, calls=%fused_computation.99 | convolution fusion | flops 3359375360 | bytes 13772800 | tf_op jit(solution)/shard_map/dot_general | solution.py:91
  217.1 31.9 %all-gather.32.cloned.1.call-done = bf16[1,1024,1280]{2,1,0:T(8,128)(2,1)} async-done(((bf16[1,256,1280]{2,1,0:T(8,128)(2,1)}), bf16[1,1024,1280]{2,1,0:T(8,128)(2,1)}) %all-gather.32.cloned.1.call-update) | async-done | bytes 2621456 | tf_op jit(solution)/shard_map/all_gather | solution.py:103
  248.9 40.4 %all-gather.30.cloned.1.call-done = bf16[1,1280,1280]{2,1,0:T(8,128)(2,1)} async-done(((bf16[1,160,1280]{2,1,0:T(8,128)(2,1)}), bf16[1,1280,1280]{2,1,0:T(8,128)(2,1)}) %all-gather.30.cloned.1.call-update) | async-done | bytes 3276816 | tf_op jit(solution)/shard_map/all_gather | solution.py:103
  289.3 8.9 %convert_reduce_fusion.1 = (f32[1280]{0:T(1024)S(1)}, bf16[1024,1280]{1,0:T(8,128)(2,1)S(1)}) fusion(f32[1024,1280]{1,0:T(8,128)} %fusion.55, f32[1280]{0:T(1024)S(1)} %add.171, bf16[1,1024,1280]{2,1,0:T(8,128)(2,1)} %all-gather.32.cloned.1.call-done, bf16[1,1280,1280]{2,1,0:T(8,128)(2,1)} %all-gather.30.cloned.1.call-done), kind=kOutput, calls=%fused_computation.23 | convolution fusion | flops 3372481280 | bytes 13772800 | tf_op jit(solution)/shard_map/dot_general | solution.py:99
  299.8 7.0 convolution_convert_fusion.4
  306.8 8.6 %convolution_convert_fusion.1 = bf16[1280,1280]{1,0:T(8,128)(2,1)} fusion(bf16[1024,1280]{1,0:T(8,128)(2,1)} %copy-done.36, f32[1024,1280]{1,0:T(8,128)} %subtract_multiply_fusion, f32[1280]{0:T(1024)S(1)} %reshape.460, f32[1280]{0:T(1024)S(1)} %reshape.459), kind=kOutput, calls=%fused_computation.12 | convolution fusion | flops 3361013760 | bytes 11151360 | tf_op jit(solution)/shard_map/dot_general | solution.py:95
  315.6 30.9 %reduce-scatter.12.cloned.1.call-done = bf16[256,1280]{1,0:T(8,128)(2,1)} async-done(((bf16[1024,1280]{1,0:T(8,128)(2,1)}), bf16[256,1280]{1,0:T(8,128)(2,1)}) %reduce-scatter.12.cloned.1.call-update) | async-done | bytes 655376 | tf_op jit(solution)/shard_map/reduce_scatter | solution.py:107
  352.8 3.5 all-to-all-start
  356.4 8.9 %convolution_convert_fusion = bf16[1280,1280]{1,0:T(8,128)(2,1)} fusion(bf16[1,1024,1280]{2,1,0:T(8,128)(2,1)} %all-gather.32.cloned.1.call-done, f32[1024,1280]{1,0:T(8,128)} %fusion.55, f32[1280]{0:T(1024)S(1)} %add.171), kind=kOutput, calls=%fused_computation.11 | convolution fusion | flops 3366256640 | bytes 11146240 | tf_op jit(solution)/shard_map/dot_general | solution.py:95
  366.8 11.7 %multiply_reduce_fusion = (f32[4,1024]{1,0:T(4,128)S(1)}, f32[4,1024,1024]{1,2,0:T(8,128)}) fusion(f32[4,1024,1024]{1,2,0:T(8,128)} %get-tuple-element.64, f32[4,1024]{1,0:T(4,128)S(1)} %log_add_fusion, bf16[1024,4,80]{0,2,1:T(8,128)(2,1)S(1)} %reshape.443, f32[1024,3,4,80]{0,3,2,1:T(8,128)} %bitcast.144), kind=kOutput, calls=%fused_computation.1 | convolution fusion | flops 683667456 | bytes 34897920 | tf_op jit(solution)/shard_map/qhd,khd->hqk/dot_general | solution.py:82
  378.5 12.2 %multiply_convert_fusion = bf16[4,1024,1024]{1,2,0:T(8,128)(2,1)S(1)} fusion(f32[4,1024,1024]{1,2,0:T(8,128)} %get-tuple-element.68, f32[4,1024,1024]{1,2,0:T(8,128)} %get-tuple-element.64, f32[4,1024]{1,0:T(4,128)S(1)} %get-tuple-element.67, f32[4,1024]{1,0:T(4,128)S(1)} %log_add_fusion), kind=kLoop, calls=%fused_computation | loop fusion | flops 16777216 | bytes 41975808 | tf_op jit(solution)/shard_map/convert_element_type | solution.py:84
  398.0 4.1 fusion.52
  405.0 4.3 convolution_convert_fusion.3
  409.6 7.1 convolution_convert_fusion.2
  416.8 9.3 %convolution_convert_fusion.5 = bf16[1024,1280]{1,0:T(8,128)(2,1)} fusion(bf16[1,1280,1280]{2,1,0:T(8,128)(2,1)} %all-gather.30.cloned.1.call-done, f32[1024,1280]{1,0:T(8,128)} %fusion.55, f32[1280]{0:T(1024)S(1)} %add.171), kind=kOutput, calls=%fused_computation.37 | convolution fusion | flops 3365928960 | bytes 11146240 | tf_op jit(solution)/shard_map/dot_general | solution.py:91
  426.4 12.8 %all_to_all.35 = bf16[256,4,320]{0,2,1:T(8,128)(2,1)S(1)} all-to-all(bf16[256,4,320]{0,2,1:T(8,128)(2,1)S(1)} %bitcast.146), channel_id=1, replica_groups=mesh['seq'=4,'fsdp'=8] {'seq'}, dimensions={1} | all-to-all | bytes 1310720 | tf_op jit(solution)/shard_map/all_to_all | solution.py:201
  439.3 4.2 convolution_convert_fusion.6
  445.0 4.6 fusion.8
  450.4 24.8 %reduce-scatter.14.cloned.1.call-done = bf16[256,1280]{1,0:T(8,128)(2,1)} async-done(((bf16[1024,1280]{1,0:T(8,128)(2,1)}), bf16[256,1280]{1,0:T(8,128)(2,1)}) %reduce-scatter.14.cloned.1.call-update) | async-done | bytes 655376 | tf_op jit(solution)/shard_map/reduce_scatter | solution.py:107
  478.3 31.0 %reduce-scatter.22.cloned.1.call-done = bf16[160,960]{1,0:T(8,128)(2,1)} async-done(((bf16[1280,960]{1,0:T(8,128)(2,1)}), bf16[160,960]{1,0:T(8,128)(2,1)}) %reduce-scatter.22.cloned.1.call-update) | async-done | bytes 307216 | tf_op jit(solution)/shard_map/reduce_scatter | solution.py:107
  509.4 47.5 %reduce-scatter.10.cloned.1.call-done = bf16[256,1280]{1,0:T(8,128)(2,1)} async-done(((bf16[1024,1280]{1,0:T(8,128)(2,1)}), bf16[256,1280]{1,0:T(8,128)(2,1)}) %reduce-scatter.10.cloned.1.call-update) | async-done | bytes 655376 | tf_op jit(solution)/shard_map/reduce_scatter | solution.py:107
  559.4 26.6 %reduce-scatter.16.cloned.1.call-done = bf16[160,320]{1,0:T(8,128)(2,1)} async-done(((bf16[1280,320]{1,0:T(8,128)(2,1)}), bf16[160,320]{1,0:T(8,128)(2,1)}) %reduce-scatter.16.cloned.1.call-update) | async-done | bytes 102416 | tf_op jit(solution)/shard_map/reduce_scatter | solution.py:107
  585.9 11.3 %all-gather.6 = bf16[4,320,160]{1,2,0:T(8,128)(2,1)S(1)} all-gather(bf16[1,320,160]{1,2,0:T(8,128)(2,1)} %bitcast.153), channel_id=1, replica_groups=mesh['seq'=4,'fsdp'=8] {'seq'}, dimensions={0}, use_global_device_ids=true | all-gather | bytes 512000 | tf_op jit(solution)/shard_map/all_gather | solution.py:103
  599.0 24.3 %all-gather.36.cloned.1.call-done = bf16[640,1280]{1,0:T(8,128)(2,1)} async-done(((bf16[160,1280]{1,0:T(8,128)(2,1)}), bf16[640,1280]{1,0:T(8,128)(2,1)}) %all-gather.36.cloned.1.call-update) | async-done | bytes 1638416 | tf_op jit(solution)/shard_map/all_gather | solution.py:103
  623.3 5.9 reshape.466
  629.2 8.2 %copy.108 = f32[160,8,4,160]{3,2,1,0:T(4,128)} copy(f32[160,8,4,160]{3,1,0,2:T(8,128)} %bitcast.139) | data formatting | bytes 6553600 | tf_op jit(solution)/shard_map/convert_element_type | solution.py:243
  637.4 7.7 reshape.464
  645.1 11.3 %all-gather.26.cloned.1.call-done = bf16[640,1280]{1,0:T(8,128)(2,1)} async-done(((bf16[160,1280]{1,0:T(8,128)(2,1)}), bf16[640,1280]{1,0:T(8,128)(2,1)}) %all-gather.26.cloned.1.call-update) | async-done | bytes 1638416 | tf_op jit(solution)/shard_map/all_gather | solution.py:103
  656.4 3.4 convert_element_type.317
  659.8 3.5 fusion.39
  663.3 46.5 %all-reduce.4.cloned.1.call-done = f32[8,2080]{1,0:T(8,128)} async-done(((f32[8,2080]{1,0:T(8,128)}), f32[8,2080]{1,0:T(8,128)}) %all-reduce.4.cloned.1.call-update) | async-done | bytes 66576
  711.4 10.2 %psum.7 = f32[1,2080]{1,0:T(1,128)S(1)} all-reduce(f32[1,2080]{1,0:T(1,128)S(1)} %constant_dynamic-slice_fusion.1), channel_id=1, replica_groups=mesh['seq'=4,'fsdp'=8] {'seq'}, use_global_device_ids=true, to_apply=%region_23.24 | all-reduce | flops 2080 | bytes 16640 | tf_op jit(solution)/shard_map/psum | solution.py:235
  723.5 18.5 %all-gather.34.cloned.1.call-done = bf16[640,960]{1,0:T(8,128)(2,1)} async-done(((bf16[160,960]{1,0:T(8,128)(2,1)}), bf16[640,960]{1,0:T(8,128)(2,1)}) %all-gather.34.cloned.1.call-update) | async-done | bytes 1228816 | tf_op jit(solution)/shard_map/all_gather | solution.py:103
  744.1 4.1 reshape.465
  748.2 6.4 copy.104
  754.6 4.4 reshape.463
  (213 shorter events, 66.3 us)
Async XLA Ops:
  7.2 125.0 %copy-start = (bf16[640,1280]{1,0:T(8,128)(2,1)S(1)}, bf16[640,1280]{1,0:T(8,128)(2,1)}, u32[]{:S(2)}) copy-start(bf16[640,1280]{1,0:T(8,128)(2,1)} %param.31) | copy-start | bytes 4915204
  7.2 19.1 %copy-start.22 = (u32[32]{0:T(128)S(1)}, u32[32]{0:T(128)}, u32[]{:S(2)}) copy-start(u32[32]{0:T(128)} %constant.74) | copy-start | bytes 388
  7.2 10.5 %copy-start.24 = (s32[1,256]{1,0:T(1,128)S(1)}, s32[1,256]{1,0:T(1,128)}, u32[]{:S(2)}) copy-start(s32[1,256]{1,0:T(1,128)} %param.20) | copy-start | bytes 3076
  7.2 10.5 %copy-start.25 = (s32[1,256]{1,0:T(1,128)S(1)}, s32[1,256]{1,0:T(1,128)}, u32[]{:S(2)}) copy-start(s32[1,256]{1,0:T(1,128)} %param.19) | copy-start | bytes 3076
  7.2 10.5 %copy-start.26 = (s32[1,256]{1,0:T(1,128)S(1)}, s32[1,256]{1,0:T(1,128)}, u32[]{:S(2)}) copy-start(s32[1,256]{1,0:T(1,128)} %param.18) | copy-start | bytes 3076
  7.2 20.3 %copy-start.33 = (bf16[160]{0:T(256)(128)(2,1)S(1)}, bf16[160]{0:T(256)(128)(2,1)}, u32[]{:S(2)}) copy-start(bf16[160]{0:T(256)(128)(2,1)} %param.32) | copy-start | bytes 964
  7.3 20.3 %copy-start.23 = (bf16[640]{0:T(1024)(128)(2,1)S(1)}, bf16[640]{0:T(1024)(128)(2,1)}, u32[]{:S(2)}) copy-start(bf16[640]{0:T(1024)(128)(2,1)} %param.30) | copy-start | bytes 3844
  7.3 20.3 %copy-start.32 = (bf16[160]{0:T(256)(128)(2,1)S(1)}, bf16[160]{0:T(256)(128)(2,1)}, u32[]{:S(2)}) copy-start(bf16[160]{0:T(256)(128)(2,1)} %param.28) | copy-start | bytes 964
  7.3 20.3 %copy-start.31 = (bf16[160]{0:T(256)(128)(2,1)S(1)}, bf16[160]{0:T(256)(128)(2,1)}, u32[]{:S(2)}) copy-start(bf16[160]{0:T(256)(128)(2,1)} %param.27) | copy-start | bytes 964
  7.3 20.3 %copy-start.30 = (bf16[160]{0:T(256)(128)(2,1)S(1)}, bf16[160]{0:T(256)(128)(2,1)}, u32[]{:S(2)}) copy-start(bf16[160]{0:T(256)(128)(2,1)} %param.26) | copy-start | bytes 964
  7.3 20.3 %copy-start.27 = (bf16[480]{0:T(512)(128)(2,1)S(1)}, bf16[480]{0:T(512)(128)(2,1)}, u32[]{:S(2)}) copy-start(bf16[480]{0:T(512)(128)(2,1)} %param.24) | copy-start | bytes 2884
  7.3 20.3 %copy-start.29 = (bf16[160]{0:T(256)(128)(2,1)S(1)}, bf16[160]{0:T(256)(128)(2,1)}, u32[]{:S(2)}) copy-start(bf16[160]{0:T(256)(128)(2,1)} %param.22) | copy-start | bytes 964
  7.3 20.3 %copy-start.28 = (bf16[160]{0:T(256)(128)(2,1)S(1)}, bf16[160]{0:T(256)(128)(2,1)}, u32[]{:S(2)}) copy-start(bf16[160]{0:T(256)(128)(2,1)} %param.21) | copy-start | bytes 964
  7.3 47.8 %all-gather.28.cloned.1.call-start = ((), (), s32[]{:S(2)}) async-start(), calls=%async_computation.20 | async-start | bytes 3276800 | tf_op jit(solution)/shard_map/all_gather | solution.py:103
  8.1 77.7 %all-gather.18.cloned.1.call-start = ((), (), s32[]{:S(2)}) async-start(), calls=%async_computation.9 | async-start | bytes 2949120 | tf_op jit(solution)/shard_map/all_gather | solution.py:103
  16.9 116.8 %all-gather.22.cloned.1.call-start = ((), (), s32[]{:S(2)}) async-start(), calls=%async_computation.11 | async-start | bytes 3686400 | tf_op jit(solution)/shard_map/all_gather | solution.py:103
  17.6 149.8 %all-gather.20.cloned.1.call-start = ((), (), s32[]{:S(2)}) async-start(), calls=%async_computation.10 | async-start | bytes 3276800 | tf_op jit(solution)/shard_map/all_gather | solution.py:103
  91.5 18.5 %copy-start.4 = (f32[1024,960]{0,1:T(8,128)}, f32[1024,960]{0,1:T(8,128)S(1)}, u32[]{:S(2)}) copy-start(f32[1024,960]{0,1:T(8,128)S(1)} %broadcast_add_fusion) | copy-start | bytes 11796484
  94.1 7.7 %copy-start.6 = (bf16[1024,4,80]{0,2,1:T(8,128)(2,1)}, bf16[1024,4,80]{0,2,1:T(8,128)(2,1)S(1)}, u32[]{:S(2)}) copy-start(bf16[1024,4,80]{0,2,1:T(8,128)(2,1)S(1)} %get-tuple-element.26) | copy-start | bytes 1966084
  94.1 7.7 %copy-start.8 = (bf16[1024,4,80]{0,2,1:T(8,128)(2,1)}, bf16[1024,4,80]{0,2,1:T(8,128)(2,1)S(1)}, u32[]{:S(2)}) copy-start(bf16[1024,4,80]{0,2,1:T(8,128)(2,1)S(1)} %get-tuple-element.27) | copy-start | bytes 1966084
  118.9 88.8 %all-gather.24.cloned.1.call-start = ((), (), s32[]{:S(2)}) async-start(), calls=%async_computation.12 | async-start | bytes 3686400 | tf_op jit(solution)/shard_map/all_gather | solution.py:103
  131.5 117.4 %all-gather.32.cloned.1.call-start = ((), (), s32[]{:S(2)}) async-start(), calls=%async_computation.22 | async-start | bytes 3276800 | tf_op jit(solution)/shard_map/all_gather | solution.py:103
  132.1 157.2 %all-gather.30.cloned.1.call-start = ((), (), s32[]{:S(2)}) async-start(), calls=%async_computation.21 | async-start | bytes 3686400 | tf_op jit(solution)/shard_map/all_gather | solution.py:103
  133.0 213.6 %reduce-scatter.12.cloned.1.call-start = ((), (), s32[]{:S(2)}) async-start(), calls=%async_computation.14 | async-start | bytes 3276800 | tf_op jit(solution)/shard_map/reduce_scatter | solution.py:107
  306.8 136.9 %reduce-scatter.18.cloned.1.call-start = ((), (), s32[]{:S(2)}) async-start(), calls=%async_computation.17 | async-start | bytes 3686400 | tf_op jit(solution)/shard_map/reduce_scatter | solution.py:107
  315.5 33.2 %copy-start.5 = (bf16[1,256,1280]{2,1,0:T(8,128)(2,1)S(1)}, bf16[1,256,1280]{2,1,0:T(8,128)(2,1)}, u32[]{:S(2)}) copy-start(bf16[1,256,1280]{2,1,0:T(8,128)(2,1)} %param.33) | copy-start | bytes 1966084
  346.5 4.2 copy-start.34
  352.8 13.0 %all-to-all-start = ((bf16[256,4,320]{0,2,1:T(8,128)(2,1)}), bf16[256,4,320]{0,2,1:T(8,128)(2,1)S(1)}, u32[]{:S(2)}, u32[]{:S(2)}) async-start(bf16[256,4,320]{0,2,1:T(8,128)(2,1)} %bitcast.17), calls=%async_computation.2 | async-start | bytes 1310720 | tf_op jit(solution)/shard_map/all_to_all | solution.py:200
  356.3 87.9 %reduce-scatter.20.cloned.1.call-start = ((), (), s32[]{:S(2)}) async-start(), calls=%async_computation.18 | async-start | bytes 3686400 | tf_op jit(solution)/shard_map/reduce_scatter | solution.py:107
  365.3 109.9 %reduce-scatter.14.cloned.1.call-start = ((), (), s32[]{:S(2)}) async-start(), calls=%async_computation.15 | async-start | bytes 3276800 | tf_op jit(solution)/shard_map/reduce_scatter | solution.py:107
  366.8 11.7 %copy-start.11 = (bf16[1024,4,80]{0,2,1:T(8,128)(2,1)}, bf16[1024,4,80]{0,2,1:T(8,128)(2,1)S(1)}, u32[]{:S(2)}) copy-start(bf16[1024,4,80]{0,2,1:T(8,128)(2,1)S(1)} %reshape.443) | copy-start | bytes 1966084
  378.5 12.2 %copy-start.9 = (bf16[1024,4,80]{0,2,1:T(8,128)(2,1)S(1)}, bf16[1024,4,80]{0,2,1:T(8,128)(2,1)}, u32[]{:S(2)}) copy-start(bf16[1024,4,80]{0,2,1:T(8,128)(2,1)} %copy-done.8) | copy-start | bytes 1966084
  390.7 7.2 slice-start
  390.7 7.2 slice-start.1
  393.4 4.5 slice-start.2
  398.0 4.1 copy-start.19
  409.3 100.0 %reduce-scatter.22.cloned.1.call-start = ((), (), s32[]{:S(2)}) async-start(), calls=%async_computation.25 | async-start | bytes 2949120 | tf_op jit(solution)/shard_map/reduce_scatter | solution.py:107
  416.7 9.5 %copy-start.18 = (bf16[256,1280]{1,0:T(8,128)(2,1)S(1)}, bf16[256,1280]{1,0:T(8,128)(2,1)}, u32[]{:S(2)}) copy-start(bf16[256,1280]{1,0:T(8,128)(2,1)} %copy-done.17) | copy-start | bytes 1966084
  416.7 140.1 %reduce-scatter.10.cloned.1.call-start = ((), (), s32[]{:S(2)}) async-start(), calls=%async_computation.13 | async-start | bytes 3276800 | tf_op jit(solution)/shard_map/reduce_scatter | solution.py:107
  426.1 159.8 %reduce-scatter.16.cloned.1.call-start = ((), (), s32[]{:S(2)}) async-start(), calls=%async_computation.16 | async-start | bytes 1105920 | tf_op jit(solution)/shard_map/reduce_scatter | solution.py:107
  443.6 179.7 %all-gather.36.cloned.1.call-start = ((), (), s32[]{:S(2)}) async-start(), calls=%async_computation.24 | async-start | bytes 2048000 | tf_op jit(solution)/shard_map/all_gather | solution.py:103
  444.2 212.2 %all-gather.26.cloned.1.call-start = ((), (), s32[]{:S(2)}) async-start(), calls=%async_computation.19 | async-start | bytes 2048000 | tf_op jit(solution)/shard_map/all_gather | solution.py:103
  444.8 265.1 %all-reduce.4.cloned.1.call-start = ((), (), s32[]{:S(2)}) async-start(), calls=%async_computation.26 | async-start | bytes 139264
  445.0 33.2 %copy-start.21 = (f32[8,160]{1,0:T(8,128)S(1)}, f32[8,160]{1,0:T(8,128)}, u32[]{:S(2)}) copy-start(f32[8,160]{1,0:T(8,128)} %get-tuple-element.44) | copy-start | bytes 15364
  478.1 263.9 %all-gather.34.cloned.1.call-start = ((), (), s32[]{:S(2)}) async-start(), calls=%async_computation.23 | async-start | bytes 1638400 | tf_op jit(solution)/shard_map/all_gather | solution.py:103
  645.1 14.7 %copy-start.10 = (bf16[256,1280]{1,0:T(8,128)(2,1)S(1)}, bf16[256,1280]{1,0:T(8,128)(2,1)}, u32[]{:S(2)}) copy-start(bf16[256,1280]{1,0:T(8,128)(2,1)} %reduce-scatter.12.cloned.1.call-done) | copy-start | bytes 1966084
  645.1 14.7 %copy-start.16 = (bf16[256,1280]{1,0:T(8,128)(2,1)S(1)}, bf16[256,1280]{1,0:T(8,128)(2,1)}, u32[]{:S(2)}) copy-start(bf16[256,1280]{1,0:T(8,128)(2,1)} %reduce-scatter.14.cloned.1.call-done) | copy-start | bytes 1966084
  748.2 10.8 %copy-start.1 = (bf16[640,1280]{1,0:T(8,128)(2,1)S(1)}, bf16[640,1280]{1,0:T(8,128)(2,1)}, u32[]{:S(2)}) copy-start(bf16[640,1280]{1,0:T(8,128)(2,1)} %param.31) | copy-start | bytes 4915204
  (12 other events, 24.6 us)
Sparse Core Ops, SparseCore 0:
  10.0 40.6 all-gather.27
  52.9 32.8 all-gather.17
  87.4 38.1 all-gather.21
  127.8 39.5 all-gather.19
  169.5 38.1 all-gather.23
  209.4 39.5 all-gather.31
  251.1 38.1 all-gather.29
  306.9 39.5 reduce-scatter.11
  349.4 38.2 reduce-scatter.17
  390.4 40.2 reduce-scatter.19
  433.7 41.4 reduce-scatter.13
  477.4 31.9 reduce-scatter.21
  512.4 44.4 reduce-scatter.9
  559.6 26.2 reduce-scatter.15
  587.6 35.6 all-gather.35
  625.0 31.3 all-gather.25
  659.2 50.6 all-reduce.3
  711.5 30.4 all-gather.33
